TPU v7x, 128 devices: a whole 4x4x4 slice. The times are simulated.
128 devices in a mesh: seq: 16 (over z, y_lo, core), head: 8 (over x, y_hi).
Axes of the slice: x: 4, y: 4 (y_hi: 2, y_lo: 2; y = y_hi * 2 + y_lo), z: 4, core: 2. Of those that a mesh axis runs over, the one named last changes fastest.
Arguments:
- tokens: bfloat16 [128, 512, 1024], P('seq'), may hold values from -36 to 36
- lengths: int32 [128], P('seq'), may hold values from 1 to 512, 32768 in all
- attn_in: float32 [1024, 3, 1024], P(('seq', 'head')), may hold values from -0.4 to 0.4
- attn_out: float32 [1024, 1024], P(None, ('seq', 'head')), may hold values from -0.1875 to 0.1875
- mlp_in: float32 [1024, 4096], P(('seq', 'head')), may hold values from -0.1875 to 0.1875
- mlp_out: float32 [4096, 1024], P(None, ('seq', 'head')), may hold values from -0.09375 to 0.09375
- norm_gain: float32 [2, 1024], replicated, may hold values from 0.5 to 1.5
- norm_shift: float32 [2, 1024], replicated, may hold values from -3 to 3
Outputs:
- encoded: bfloat16 [128, 512, 1024], P('seq', 'head')
- key_cache: bfloat16 [128, 512, 1024], P('seq', None, 'head')
- value_cache: bfloat16 [128, 512, 1024], P('seq', None, 'head')
Inputs may be any that keep to these rules, and one draw needn't show every extreme that they name: `lengths`: some prompt has exactly 512 tokens.
All inputs are finite; a program needn't handle non-finite values. No bound on the sum of `lengths` on one device may be relied on, other than what follows from the above.
Results may differ from a plain program's by a relative error of at most 0.02.
Values may be sent and summed in bfloat16 or wider, within the bound.
A program may use at most 128 MiB of HBM per device.

v0:
```python
import math

import jax
import jax.numpy as jnp
from jax import lax
from jax.sharding import PartitionSpec as P

DH = 64


EPSILON = 1e-05


def layer_norm(values, gain, shift):
    center = values - jnp.mean(values, axis=-1, keepdims=True)
    spread = jnp.mean(center * center, axis=-1, keepdims=True)
    return center * lax.rsqrt(spread + EPSILON) * gain + shift


def shards(tokens, lengths, attn_in, attn_out, mlp_in, mlp_out, norm_gain, norm_shift):
    heads_axis = lax.axis_size("head")
    head_index = lax.axis_index("head")
    prompts = tokens.shape[0]
    seq_len = tokens.shape[1]
    model_width = tokens.shape[2]
    hidden_width = mlp_in.shape[1]
    block_width = model_width // heads_axis
    hidden_block = hidden_width // heads_axis
    local_heads = block_width // DH
    in_cast = attn_in.astype(jnp.bfloat16)
    up_cast = mlp_in.astype(jnp.bfloat16)
    out_cast = attn_out.astype(jnp.bfloat16)
    down_cast = mlp_out.astype(jnp.bfloat16)
    whole_in, whole_up = (
        lax.all_gather(in_cast, ("seq", "head"), axis=0, tiled=True),
        lax.all_gather(up_cast, ("seq", "head"), axis=0, tiled=True),
    )
    whole_out, whole_down = (
        lax.all_gather(out_cast, ("seq", "head"), axis=1, tiled=True),
        lax.all_gather(down_cast, ("seq", "head"), axis=1, tiled=True),
    )
    qkv_weight = lax.dynamic_slice_in_dim(whole_in, head_index * block_width, block_width, 2)
    up_weight = lax.dynamic_slice_in_dim(whole_up, head_index * hidden_block, hidden_block, 1)
    proj_weight = lax.dynamic_slice_in_dim(whole_out, head_index * block_width, block_width, 0)
    down_weight = lax.dynamic_slice_in_dim(whole_down, head_index * hidden_block, hidden_block, 0)
    projected = jnp.einsum(
        "pld,dte->plte", tokens, qkv_weight, preferred_element_type=jnp.float32
    ).astype(jnp.bfloat16)
    positions = jnp.arange(seq_len, dtype=jnp.int32)
    inside = positions[None, :] < lengths[:, None]
    key_part = projected[:, :, 1]
    value_part = projected[:, :, 2]
    queries = projected[:, :, 0].reshape(prompts, seq_len, local_heads, DH)
    key_heads = key_part.reshape(prompts, seq_len, local_heads, DH)
    value_heads = value_part.reshape(prompts, seq_len, local_heads, DH)
    scores = jnp.einsum(
        "pqhd,pkhd->phqk", queries, key_heads, preferred_element_type=jnp.float32
    ) * (1.0 / math.sqrt(DH))
    scores = jnp.where(inside[:, None, None, :], scores, -1e30)
    row_peak = jnp.max(scores, axis=-1, keepdims=True)
    raised = jnp.exp(scores - row_peak)
    weights = (raised / jnp.sum(raised, axis=-1, keepdims=True)).astype(jnp.bfloat16)
    context = jnp.einsum(
        "phqk,pkhd->pqhd", weights, value_heads, preferred_element_type=jnp.float32
    )
    context = context.astype(jnp.bfloat16).reshape(prompts, seq_len, block_width)
    key_cache = jnp.where(inside[:, :, None], key_part, jnp.zeros_like(key_part))
    value_cache = jnp.where(inside[:, :, None], value_part, jnp.zeros_like(value_part))
    row_count = seq_len // heads_axis
    row_start = head_index * row_count
    attn_partial = jnp.einsum(
        "pld,de->ple", context, proj_weight, preferred_element_type=jnp.float32
    )
    attn_total = lax.psum(attn_partial.astype(jnp.bfloat16), "head").astype(jnp.float32)
    normed = layer_norm(
        tokens.astype(jnp.float32) + attn_total, norm_gain[0], norm_shift[0]
    ).astype(jnp.bfloat16)
    hidden = jax.nn.gelu(
        jnp.einsum("pld,df->plf", normed, up_weight, preferred_element_type=jnp.float32),
        approximate=False,
    ).astype(jnp.bfloat16)
    mlp_partial = jnp.einsum("plf,fe->ple", hidden, down_weight, preferred_element_type=jnp.float32)
    mlp_total = lax.psum(mlp_partial.astype(jnp.bfloat16), "head").astype(jnp.float32)
    mlp_rows = lax.dynamic_slice_in_dim(mlp_total, row_start, row_count, 1)
    normed_rows = lax.dynamic_slice_in_dim(normed, row_start, row_count, 1)
    finished = layer_norm(normed_rows.astype(jnp.float32) + mlp_rows, norm_gain[1], norm_shift[1])
    inside_rows = lax.dynamic_slice_in_dim(inside, row_start, row_count, 1)
    encoded = jnp.where(inside_rows[:, :, None], finished, 0.0).astype(jnp.bfloat16)
    return (encoded, key_cache, value_cache)


def solution(mesh):
    in_specs = (
        P("seq", None, None),
        P("seq"),
        P(("seq", "head"), None, None),
        P(None, ("seq", "head")),
        P(("seq", "head"), None),
        P(None, ("seq", "head")),
        P(),
        P(),
    )
    out_specs = (P("seq", "head", None), P("seq", None, "head"), P("seq", None, "head"))
    return jax.shard_map(shards, mesh=mesh, in_specs=in_specs, out_specs=out_specs, check_vma=False)
```

profile of v0, /device:TPU:1, one launch (start us, length us, event | category | flops | bytes accessed | tf_op | source)
XLA Modules:
  0.0 1993.4 jit_solution(4811427423601753310)
XLA Ops:
  7.2 0.0 all-gather.5.cloned.1.call-start
  7.2 1.5 convert_element_type.55
  8.7 0.0 all-gather.5.cloned.1.call-update
  8.8 0.0 all-gather.7.cloned.1.call-start
  8.8 1.4 convert_element_type.61
  10.2 0.0 all-gather.7.cloned.1.call-update
  10.2 0.0 all-reduce.3.cloned.1.call-start
  10.2 0.7 iota_compare_fusion
  11.0 314.5 %all-gather.5.cloned.1.call-done = bf16[1024,3,1024]{2,0,1:T(8,128)(2,1)} async-done(((bf16[8,3,1024]{2,0,1:T(8,128)(2,1)}), bf16[1024,3,1024]{2,0,1:T(8,128)(2,1)}) %all-gather.5.cloned.1.call-update) | async-done | bytes 6291472 | tf_op jit(solution)/shard_map/all_gather | solution.py:35
  325.5 7.1 convert_bitcast_fusion
  332.7 1.7 fusion.108
  334.4 10.7 fusion.111
  345.1 8.7 fusion.59
  353.8 275.3 %all-gather.7.cloned.1.call-done = bf16[1024,1024]{0,1:T(8,128)(2,1)} async-done(((bf16[1024,8]{0,1:T(8,128)(2,1)}), bf16[1024,1024]{0,1:T(8,128)(2,1)}) %all-gather.7.cloned.1.call-update) | async-done | bytes 2097168 | tf_op jit(solution)/shard_map/all_gather | solution.py:39
  629.1 0.0 copy-start.1
  629.1 0.0 copy-start.2
  629.1 0.0 copy-start.3
  629.1 0.0 copy-start.4
  629.2 6.9 convolution_convert_fusion
  636.1 0.0 all-reduce.3.cloned.1.call-update
  636.1 0.0 all-gather.9.cloned.1.call-start
  636.1 0.0 copy-done.1
  636.1 0.6 convert_element_type.66
  636.8 0.0 all-gather.9.cloned.1.call-update
  636.8 0.0 all-gather.11.cloned.1.call-start
  636.9 0.0 copy-done.2
  636.9 0.6 convert_element_type.68
  637.5 0.0 all-gather.11.cloned.1.call-update
  637.5 0.2 all-reduce.5.cloned.1.call-start
  637.8 0.0 copy-done.3
  637.8 0.0 copy-done.4
  637.8 340.4 %all-reduce.3.cloned.1.call-done = bf16[8,512,1024]{2,1,0:T(8,128)(2,1)} async-done(((bf16[8,512,1024]{2,1,0:T(8,128)(2,1)}), bf16[8,512,1024]{2,1,0:T(8,128)(2,1)}) %all-reduce.3.cloned.1.call-update) | async-done | bytes 8388624 | tf_op jit(solution)/shard_map/psum | solution.py:74
  978.3 8.0 fusion.2
  986.3 0.0 copy-start
  986.3 8.0 multiply_reduce_fusion
  994.3 0.2 copy-done
  994.6 9.3 add_convert_fusion
  1003.8 293.9 %all-gather.9.cloned.1.call-done = bf16[1024,4096]{1,0:T(8,128)(2,1)} async-done(((bf16[8,4096]{1,0:T(8,128)(2,1)}), bf16[1024,4096]{1,0:T(8,128)(2,1)}) %all-gather.9.cloned.1.call-update) | async-done | bytes 8388624 | tf_op jit(solution)/shard_map/all_gather | solution.py:36
  1297.7 14.5 fusion.54
  1312.3 300.0 %all-gather.11.cloned.1.call-done = bf16[4096,1024]{0,1:T(8,128)(2,1)} async-done(((bf16[4096,8]{0,1:T(8,128)(2,1)}), bf16[4096,1024]{0,1:T(8,128)(2,1)}) %all-gather.11.cloned.1.call-update) | async-done | bytes 8388624 | tf_op jit(solution)/shard_map/all_gather | solution.py:40
  1612.3 25.3 %convolution_convert_fusion.1 = bf16[8,512,1024]{2,1,0:T(8,128)(2,1)} fusion(f32[8,512,512]{2,1,0:T(8,128)} %get-tuple-element.22, u8[512,512]{1,0:T(8,128)(4,1)} %get-tuple-element.10, u8[512,512]{1,0:T(8,128)(4,1)} %get-tuple-element.9, bf16[4096,1024]{0,1:T(8,128)(2,1)} %all-gather.11.cloned.1.call-done, s32[]{:T(128)S(6)} %select_n.31), kind=kOutput, calls=%fused_computation.39 | convolution fusion | flops 4445962240 | bytes 18350084 | tf_op jit(solution)/shard_map/plf,fe->ple/dot_general | solution.py:82
  1637.6 0.0 all-reduce.5.cloned.1.call-update
  1637.6 0.1 constant_dynamic-slice_fusion
  1637.7 1.5 bitcast_select_fusion
  1639.2 2.3 copy.23
  1641.4 2.3 copy.24
  1643.7 335.7 %all-reduce.5.cloned.1.call-done = bf16[8,512,1024]{2,1,0:T(8,128)(2,1)} async-done(((bf16[8,512,1024]{2,1,0:T(8,128)(2,1)}), bf16[8,512,1024]{2,1,0:T(8,128)(2,1)}) %all-reduce.5.cloned.1.call-update) | async-done | bytes 8388624 | tf_op jit(solution)/shard_map/psum | solution.py:83
  1979.4 1.9 fusion.56
  1981.3 2.0 multiply_reduce_fusion.1
  1983.3 3.2 select_convert_fusion
  (6 shorter events, 0.0 us)
Async XLA Ops:
  7.2 318.4 %all-gather.5.cloned.1.call-start = ((), (), s32[]{:S(2)}) async-start(), calls=%async_computation | async-start | bytes 6340608 | tf_op jit(solution)/shard_map/all_gather | solution.py:35
  8.8 620.4 %all-gather.7.cloned.1.call-start = ((), (), s32[]{:S(2)}) async-start(), calls=%async_computation.1 | async-start | bytes 2113536 | tf_op jit(solution)/shard_map/all_gather | solution.py:39
  10.2 968.1 %all-reduce.3.cloned.1.call-start = ((), (), s32[]{:S(2)}) async-start(), calls=%async_computation.2 | async-start | bytes 16777216 | tf_op jit(solution)/shard_map/psum | solution.py:74
  629.1 7.0 copy-start.1
  629.1 7.7 copy-start.2
  629.1 8.6 copy-start.3
  629.1 8.6 copy-start.4
  636.1 661.7 %all-gather.9.cloned.1.call-start = ((), (), s32[]{:S(2)}) async-start(), calls=%async_computation.3 | async-start | bytes 8454144 | tf_op jit(solution)/shard_map/all_gather | solution.py:36
  636.8 975.5 %all-gather.11.cloned.1.call-start = ((), (), s32[]{:S(2)}) async-start(), calls=%async_computation.4 | async-start | bytes 8454144 | tf_op jit(solution)/shard_map/all_gather | solution.py:40
  637.5 1341.9 %all-reduce.5.cloned.1.call-start = ((), (), s32[]{:S(2)}) async-start(), calls=%async_computation.5 | async-start | bytes 16777216 | tf_op jit(solution)/shard_map/psum | solution.py:83
  986.3 8.3 copy-start
Sparse Core Ops, SparseCore 0:
  10.3 315.2 all-gather.4
  327.2 301.8 all-gather.6
  636.2 342.0 all-reduce.2
  980.4 317.3 all-gather.8
  1299.8 312.3 all-gather.10
  1637.7 341.5 all-reduce.4
where the time goes:
time: 2000 us; the launch traced here: 1990 us
  waiting for transfers between devices  1860 us (93%)
  matrix products  73.3 us (4%)
  other arithmetic  38.8 us (2%)
    psum x1, waiting for transfers between devices, shards(): lax.psum(attn_partial.astype(jnp.bfloat16), 'head').astype(jnp.float32)  340 us
    psum x1, waiting for transfers between devices, shards(): lax.psum(mlp_partial.astype(jnp.bfloat16), 'head').astype(jnp.float32)  336 us
    all_gather x1, waiting for transfers between devices, shards(): lax.all_gather(in_cast, ('seq', 'head'), axis=0, tiled=True)  315 us
    all_gather x1, waiting for transfers between devices, shards(): lax.all_gather(down_cast, ('seq', 'head'), axis=1, tiled=True)  300 us
    all_gather x1, waiting for transfers between devices, shards(): lax.all_gather(up_cast, ('seq', 'head'), axis=0, tiled=True)  294 us
    all_gather x1, waiting for transfers between devices, shards(): lax.all_gather(out_cast, ('seq', 'head'), axis=1, tiled=True)  275 us
  transfers between devices with their start and end apart: 6, of which 6 were waited for; matrix products, arithmetic and copies ran while one was open for 4% of the time, Pallas kernels for 0%

commit v1 on v0

--- a/solution.py
+++ b/solution.py
@@ -17,32 +17,40 @@
     return center * lax.rsqrt(spread + EPSILON) * gain + shift
 
 
+def regroup_weights(attn_in, attn_out, mlp_in, mlp_out, heads_axis):
+    rows = attn_in.shape[0]
+    model_width = attn_in.shape[2]
+    hidden_width = mlp_in.shape[1]
+    block_width = model_width // heads_axis
+    hidden_block = hidden_width // heads_axis
+    in_piece = attn_in.astype(jnp.bfloat16).reshape(rows, 3, heads_axis, block_width)
+    in_piece = jnp.transpose(in_piece, (0, 2, 1, 3)).reshape(rows, heads_axis, 3 * block_width)
+    up_piece = mlp_in.astype(jnp.bfloat16).reshape(rows, heads_axis, hidden_block)
+    out_piece = attn_out.astype(jnp.bfloat16).T.reshape(rows, heads_axis, block_width)
+    down_piece = mlp_out.astype(jnp.bfloat16).T.reshape(rows, heads_axis, hidden_block)
+    packed = jnp.concatenate([in_piece, up_piece, out_piece, down_piece], axis=2)
+    packed = lax.all_to_all(packed, "head", 1, 0, tiled=True)
+    packed = packed.reshape(rows * heads_axis, packed.shape[2])
+    whole = lax.all_gather(packed, "seq", axis=0, tiled=True)
+    edges = [0, 3 * block_width, 3 * block_width + hidden_block,
+             4 * block_width + hidden_block, 4 * block_width + 2 * hidden_block]
+    qkv_weight = whole[:, edges[0]:edges[1]].reshape(-1, 3, block_width)
+    up_weight = whole[:, edges[1]:edges[2]]
+    proj_weight_t = whole[:, edges[2]:edges[3]]
+    down_weight_t = whole[:, edges[3]:edges[4]]
+    return qkv_weight, up_weight, proj_weight_t, down_weight_t
+
+
 def shards(tokens, lengths, attn_in, attn_out, mlp_in, mlp_out, norm_gain, norm_shift):
     heads_axis = lax.axis_size("head")
     head_index = lax.axis_index("head")
     prompts = tokens.shape[0]
     seq_len = tokens.shape[1]
     model_width = tokens.shape[2]
-    hidden_width = mlp_in.shape[1]
     block_width = model_width // heads_axis
-    hidden_block = hidden_width // heads_axis
     local_heads = block_width // DH
-    in_cast = attn_in.astype(jnp.bfloat16)
-    up_cast = mlp_in.astype(jnp.bfloat16)
-    out_cast = attn_out.astype(jnp.bfloat16)
-    down_cast = mlp_out.astype(jnp.bfloat16)
-    whole_in, whole_up = (
-        lax.all_gather(in_cast, ("seq", "head"), axis=0, tiled=True),
-        lax.all_gather(up_cast, ("seq", "head"), axis=0, tiled=True),
-    )
-    whole_out, whole_down = (
-        lax.all_gather(out_cast, ("seq", "head"), axis=1, tiled=True),
-        lax.all_gather(down_cast, ("seq", "head"), axis=1, tiled=True),
-    )
-    qkv_weight = lax.dynamic_slice_in_dim(whole_in, head_index * block_width, block_width, 2)
-    up_weight = lax.dynamic_slice_in_dim(whole_up, head_index * hidden_block, hidden_block, 1)
-    proj_weight = lax.dynamic_slice_in_dim(whole_out, head_index * block_width, block_width, 0)
-    down_weight = lax.dynamic_slice_in_dim(whole_down, head_index * hidden_block, hidden_block, 0)
+    qkv_weight, up_weight, proj_weight_t, down_weight_t = regroup_weights(
+        attn_in, attn_out, mlp_in, mlp_out, heads_axis)
     projected = jnp.einsum(
         "pld,dte->plte", tokens, qkv_weight, preferred_element_type=jnp.float32
     ).astype(jnp.bfloat16)
@@ -69,7 +77,7 @@
     row_count = seq_len // heads_axis
     row_start = head_index * row_count
     attn_partial = jnp.einsum(
-        "pld,de->ple", context, proj_weight, preferred_element_type=jnp.float32
+        "pld,ed->ple", context, proj_weight_t, preferred_element_type=jnp.float32
     )
     attn_total = lax.psum(attn_partial.astype(jnp.bfloat16), "head").astype(jnp.float32)
     normed = layer_norm(
@@ -79,9 +87,10 @@
         jnp.einsum("pld,df->plf", normed, up_weight, preferred_element_type=jnp.float32),
         approximate=False,
     ).astype(jnp.bfloat16)
-    mlp_partial = jnp.einsum("plf,fe->ple", hidden, down_weight, preferred_element_type=jnp.float32)
-    mlp_total = lax.psum(mlp_partial.astype(jnp.bfloat16), "head").astype(jnp.float32)
-    mlp_rows = lax.dynamic_slice_in_dim(mlp_total, row_start, row_count, 1)
+    mlp_partial = jnp.einsum("plf,ef->ple", hidden, down_weight_t, preferred_element_type=jnp.float32)
+    mlp_rows = lax.psum_scatter(
+        mlp_partial.astype(jnp.bfloat16), "head", scatter_dimension=1, tiled=True
+    ).astype(jnp.float32)
     normed_rows = lax.dynamic_slice_in_dim(normed, row_start, row_count, 1)
     finished = layer_norm(normed_rows.astype(jnp.float32) + mlp_rows, norm_gain[1], norm_shift[1])
     inside_rows = lax.dynamic_slice_in_dim(inside, row_start, row_count, 1)

time: 2000 us -> 627 us (0.31)
  waiting for transfers between devices: 1860 us -> 490 us
    all_gather x4 -> x1, waiting for transfers between devices: 1180 us -> 35.7 us  [regroup_weights(): whole = lax.all_gather(packed, 'seq', axis=0, tiled=True)]
    psum x1 -> x0, waiting for transfers between devices: 336 us -> none  [shards(): lax.psum(mlp_partial.astype(jnp.bfloat16), 'head').astype(jnp.float32)]
    reduce_scatter x0 -> x1, waiting for transfers between devices: none -> 113 us  [shards(): lax.psum_scatter(mlp_partial.astype(jnp.bfloat16), 'head', scatter_dimens...]
  transfers between devices with their start and end apart: 6 -> 3, of which waited for: 6 -> 3; matrix products, arithmetic and copies ran while one was open for 4% -> 1% of each run, Pallas kernels for 0% -> 0%
where the time goes in v1:
time: 627 us; the launch traced here: 626 us
  waiting for transfers between devices  490 us (78%)
  matrix products  62.5 us (10%)
  other arithmetic  35.6 us (6%)
  blocking collectives  14.5 us (2%)
  between operations  13.9 us (2%)
  local copies, waits for them, and re-layouts  9.03 us (1%)
    psum x1, waiting for transfers between devices, shards(): lax.psum(attn_partial.astype(jnp.bfloat16), 'head').astype(jnp.float32)  341 us
    reduce_scatter x1, waiting for transfers between devices, shards(): lax.psum_scatter(mlp_partial.astype(jnp.bfloat16), 'head', scatter_dimens...  113 us
    all_gather x1, waiting for transfers between devices, regroup_weights(): whole = lax.all_gather(packed, 'seq', axis=0, tiled=True)  35.7 us
    dot_general x1, matrix products, shards(): jnp.einsum('plf,ef->ple', hidden, down_weight_t, preferred_element_type=j...  23.6 us
    all_to_all x1, blocking collectives, regroup_weights(): packed = lax.all_to_all(packed, 'head', 1, 0, tiled=True)  14.5 us
  transfers between devices with their start and end apart: 3, of which 3 were waited for; matrix products, arithmetic and copies ran while one was open for 1% of the time, Pallas kernels for 0%

profile of v1, /device:TPU:1, one launch (start us, length us, event | category | flops | bytes accessed | tf_op | source)
XLA Modules:
  0.0 626.0 jit_solution(456908509169203489)
XLA Ops:
  7.2 0.0 all-gather.2.cloned.1.call-start
  7.2 0.8 convert_bitcast_fusion.2
  8.0 0.9 copy_bitcast_fusion
  8.9 0.9 convert_element_type.56
  9.8 0.9 convert_element_type.58
  10.7 14.5 %all_to_all.15 = bf16[8,8,1536]{2,0,1:T(8,128)(2,1)} all-to-all(bf16[8,8,1536]{2,0,1:T(8,128)(2,1)S(1)} %pad_maximum_fusion), channel_id=1, replica_groups=mesh['seq'=16,'head'=8] {'head'}, dimensions={1} | all-to-all | bytes 393216 | tf_op jit(solution)/shard_map/all_to_all | solution.py:32
  25.2 0.0 all-gather.2.cloned.1.call-update
  25.2 0.0 all-reduce.2.cloned.1.call-start
  25.3 0.7 iota_compare_fusion
  26.0 35.7 %all-gather.2.cloned.1.call-done = bf16[1024,1536]{1,0:T(8,128)(2,1)} async-done(((bf16[64,1536]{1,0:T(8,128)(2,1)}), bf16[1024,1536]{1,0:T(8,128)(2,1)}) %all-gather.2.cloned.1.call-update) | async-done | bytes 3145744 | tf_op jit(solution)/shard_map/all_gather | solution.py:34
  61.7 1.2 slice.44
  62.9 1.2 copy.12
  64.0 7.1 %convert_bitcast_fusion = bf16[8,512,3,128]{1,3,0,2:T(8,128)(2,1)S(1)} fusion(bf16[1024,3,128,1]{0,2,3,1:T(8,128)(2,1)} %bitcast.69, bf16[8,512,1024]{2,1,0:T(8,128)(2,1)} %param.8), kind=kOutput, calls=%fused_computation.71 | convolution fusion | flops 3222798336 | bytes 12320768 | tf_op jit(solution)/shard_map/pld,dte->plte/dot_general | solution.py:54
  71.1 1.8 fusion.96
  72.9 10.7 %fusion.99 = (f32[8,2,512]{2,1,0:T(2,128)S(1)}, f32[8,2,512,512]{2,3,1,0:T(8,128)}) fusion(pred[8,512]{1,0:T(8,128)(4,1)S(1)} %iota_compare_fusion, bf16[8,512,2,64]{1,3,2,0:T(8,128)(2,1)} %bitcast.68, bf16[8,512,2,64]{1,3,2,0:T(8,128)(2,1)} %bitcast.67), kind=kOutput, calls=%fused_computation.135 | convolution fusion | flops 553648640 | bytes 18911232 | tf_op jit(solution)/shard_map/sub | solution.py:69
  83.7 7.7 %fusion.59 = bf16[8,2,64,512]{3,2,1,0:T(8,128)(2,1)S(1)} fusion(bf16[8,512,2,64]{1,3,2,0:T(8,128)(2,1)} %bitcast.66, f32[8,2,512,512]{2,3,1,0:T(8,128)} %get-tuple-element.18, f32[8,2,512]{2,1,0:T(2,128)S(1)} %get-tuple-element.17), kind=kOutput, calls=%fused_computation.80 | convolution fusion | flops 545783808 | bytes 18907136 | tf_op jit(solution)/shard_map/phqk,pkhd->pqhd/dot_general | solution.py:71
  91.4 0.0 copy-start.3
  91.4 0.0 copy-start.4
  91.4 6.5 %convolution_convert_fusion = bf16[8,512,1024]{2,1,0:T(8,128)(2,1)} fusion(bf16[8,512,128]{1,2,0:T(8,128)(2,1)S(1)} %bitcast.65, bf16[1024,1536]{1,0:T(8,128)(2,1)} %all-gather.2.cloned.1.call-done), kind=kOutput, calls=%fused_computation.38 | convolution fusion | flops 1077936128 | bytes 9699328 | tf_op jit(solution)/shard_map/pld,ed->ple/dot_general | solution.py:79
  97.9 0.0 all-reduce.2.cloned.1.call-update
  97.9 0.2 reduce-scatter.2.cloned.1.call-start
  98.2 0.0 copy-done.3
  98.2 0.0 copy-done.4
  98.2 341.3 %all-reduce.2.cloned.1.call-done = bf16[8,512,1024]{2,1,0:T(8,128)(2,1)} async-done(((bf16[8,512,1024]{2,1,0:T(8,128)(2,1)}), bf16[8,512,1024]{2,1,0:T(8,128)(2,1)}) %all-reduce.2.cloned.1.call-update) | async-done | bytes 8388624 | tf_op jit(solution)/shard_map/psum | solution.py:82
  439.5 8.0 %fusion.2 = f32[8,512]{1,0:T(8,128)S(1)} fusion(bf16[8,512,1024]{2,1,0:T(8,128)(2,1)} %all-reduce.2.cloned.1.call-done, bf16[8,512,1024]{2,1,0:T(8,128)(2,1)} %param.8), kind=kLoop, calls=%fused_computation.8 | loop fusion | flops 16773120 | bytes 16793600 | tf_op jit(solution)/shard_map/reduce_sum | solution.py:15
  447.6 0.0 copy-start
  447.6 8.0 %multiply_reduce_fusion = f32[8,512]{1,0:T(8,128)S(1)} fusion(bf16[8,512,1024]{2,1,0:T(8,128)(2,1)} %all-reduce.2.cloned.1.call-done, bf16[8,512,1024]{2,1,0:T(8,128)(2,1)} %param.8, f32[8,512]{1,0:T(8,128)S(1)} %broadcast_multiply_fusion), kind=kLoop, calls=%fused_computation.2 | loop fusion | flops 25161728 | bytes 16809984 | tf_op jit(solution)/shard_map/reduce_sum | solution.py:16
  455.6 0.2 copy-done
  455.9 0.0 copy-start.2
  455.9 6.7 %add_convert_fusion = bf16[8,512,1024]{2,1,0:T(8,128)(2,1)S(1)} fusion(bf16[8,512,1024]{2,1,0:T(8,128)(2,1)S(1)} %copy-done, bf16[8,512,1024]{2,1,0:T(8,128)(2,1)} %param.8, f32[1024]{0:T(1024)S(1)} %bitcast.76, f32[1024]{0:T(1024)S(1)} %bitcast.75, f32[8,512]{1,0:T(8,128)S(1)} %add_rsqrt_fusion, f32[8,512]{1,0:T(8,128)S(1)} %broadcast_multiply_fusion), kind=kLoop, calls=%fused_computation.1 | loop fusion | flops 33554432 | bytes 25206784 | tf_op jit(solution)/shard_map/convert_element_type | solution.py:85
  462.5 0.0 copy-done.2
  462.6 0.0 copy-start.1
  462.6 6.8 %fusion.54 = (u8[512,512]{1,0:T(8,128)(4,1)S(1)}, u8[512,512]{1,0:T(8,128)(4,1)S(1)}, f32[8,512,512]{2,1,0:T(8,128)S(1)}) fusion(bf16[8,512,1024]{2,1,0:T(8,128)(2,1)S(1)} %add_convert_fusion, bf16[1024,1536]{1,0:T(8,128)(2,1)S(1)} %copy-done.2), kind=kOutput, calls=%fused_computation.76 | convolution fusion | flops 4321705984 | bytes 18350080 | tf_op jit(solution)/shard_map/pld,df->plf/dot_general | solution.py:87
  469.4 0.0 copy-done.1
  469.4 23.6 %convolution_convert_fusion.1 = bf16[8,512,1024]{2,1,0:T(8,128)(2,1)} fusion(f32[8,512,512]{2,1,0:T(8,128)S(1)} %get-tuple-element.19, u8[512,512]{1,0:T(8,128)(4,1)S(1)} %get-tuple-element.7, u8[512,512]{1,0:T(8,128)(4,1)S(1)} %get-tuple-element.6, bf16[1024,1536]{1,0:T(8,128)(2,1)S(1)} %copy-done.2), kind=kOutput, calls=%fused_computation.39 | convolution fusion | flops 4445962240 | bytes 18350080 | tf_op jit(solution)/shard_map/plf,ef->ple/dot_general | solution.py:90
  493.0 0.0 reduce-scatter.2.cloned.1.call-update
  493.0 0.1 constant_dynamic-slice_fusion
  493.1 1.5 bitcast_select_fusion
  494.6 2.3 copy.16
  496.8 2.3 copy.15
  499.1 113.2 %reduce-scatter.2.cloned.1.call-done = bf16[8,64,1024]{2,1,0:T(8,128)(2,1)} async-done(((bf16[8,512,1024]{2,1,0:T(8,128)(2,1)}), bf16[8,64,1024]{2,1,0:T(8,128)(2,1)}) %reduce-scatter.2.cloned.1.call-update) | async-done | bytes 1048592 | tf_op jit(solution)/shard_map/reduce_scatter | solution.py:91
  612.2 1.9 fusion.56
  614.1 2.0 multiply_reduce_fusion.1
  616.2 3.2 select_convert_fusion
  (7 shorter events, 0.1 us)
Async XLA Ops:
  7.2 54.5 %all-gather.2.cloned.1.call-start = ((), (), s32[]{:S(2)}) async-start(), calls=%async_computation.2 | async-start | bytes 3342336 | tf_op jit(solution)/shard_map/all_gather | solution.py:34
  25.2 414.3 %all-reduce.2.cloned.1.call-start = ((), (), s32[]{:S(2)}) async-start(), calls=%async_computation.3 | async-start | bytes 16777216 | tf_op jit(solution)/shard_map/psum | solution.py:82
  91.4 6.8 %copy-start.3 = (f32[2,1024]{1,0:T(2,128)S(1)}, f32[2,1024]{1,0:T(2,128)}, u32[]{:S(2)}) copy-start(f32[2,1024]{1,0:T(2,128)} %param.14) | copy-start | bytes 24580
  91.4 6.8 %copy-start.4 = (f32[2,1024]{1,0:T(2,128)S(1)}, f32[2,1024]{1,0:T(2,128)}, u32[]{:S(2)}) copy-start(f32[2,1024]{1,0:T(2,128)} %param.15) | copy-start | bytes 24580
  97.9 514.3 %reduce-scatter.2.cloned.1.call-start = ((), (), s32[]{:S(2)}) async-start(), calls=%async_computation.4 | async-start | bytes 9437184 | tf_op jit(solution)/shard_map/reduce_scatter | solution.py:91
  447.6 8.3 %copy-start = (bf16[8,512,1024]{2,1,0:T(8,128)(2,1)S(1)}, bf16[8,512,1024]{2,1,0:T(8,128)(2,1)}, u32[]{:S(2)}) copy-start(bf16[8,512,1024]{2,1,0:T(8,128)(2,1)} %all-reduce.2.cloned.1.call-done) | copy-start | bytes 25165828
  455.9 6.7 %copy-start.2 = (bf16[1024,1536]{1,0:T(8,128)(2,1)S(1)}, bf16[1024,1536]{1,0:T(8,128)(2,1)}, u32[]{:S(2)}) copy-start(bf16[1024,1536]{1,0:T(8,128)(2,1)} %all-gather.2.cloned.1.call-done) | copy-start | bytes 9437188
  462.6 6.8 %copy-start.1 = (bf16[8,512,1024]{2,1,0:T(8,128)(2,1)}, bf16[8,512,1024]{2,1,0:T(8,128)(2,1)S(1)}, u32[]{:S(2)}) copy-start(bf16[8,512,1024]{2,1,0:T(8,128)(2,1)S(1)} %add_convert_fusion) | copy-start | bytes 25165828
Sparse Core Ops, SparseCore 0:
  25.3 36.2 all-gather.1
  98.1 341.4 all-reduce.1
  493.1 119.0 reduce-scatter.1

commit v2 on v1

--- a/solution.py
+++ b/solution.py
@@ -79,10 +79,14 @@
     attn_partial = jnp.einsum(
         "pld,ed->ple", context, proj_weight_t, preferred_element_type=jnp.float32
     )
-    attn_total = lax.psum(attn_partial.astype(jnp.bfloat16), "head").astype(jnp.float32)
-    normed = layer_norm(
-        tokens.astype(jnp.float32) + attn_total, norm_gain[0], norm_shift[0]
+    attn_rows = lax.psum_scatter(
+        attn_partial.astype(jnp.bfloat16), "head", scatter_dimension=1, tiled=True
+    ).astype(jnp.float32)
+    token_rows = lax.dynamic_slice_in_dim(tokens, row_start, row_count, 1)
+    normed_rows = layer_norm(
+        token_rows.astype(jnp.float32) + attn_rows, norm_gain[0], norm_shift[0]
     ).astype(jnp.bfloat16)
+    normed = lax.all_gather(normed_rows, "head", axis=1, tiled=True)
     hidden = jax.nn.gelu(
         jnp.einsum("pld,df->plf", normed, up_weight, preferred_element_type=jnp.float32),
         approximate=False,
@@ -91,7 +95,6 @@
     mlp_rows = lax.psum_scatter(
         mlp_partial.astype(jnp.bfloat16), "head", scatter_dimension=1, tiled=True
     ).astype(jnp.float32)
-    normed_rows = lax.dynamic_slice_in_dim(normed, row_start, row_count, 1)
     finished = layer_norm(normed_rows.astype(jnp.float32) + mlp_rows, norm_gain[1], norm_shift[1])
     inside_rows = lax.dynamic_slice_in_dim(inside, row_start, row_count, 1)
     encoded = jnp.where(inside_rows[:, :, None], finished, 0.0).astype(jnp.bfloat16)

time: 627 us -> 485 us (0.77)
  waiting for transfers between devices: 490 us -> 365 us
  other arithmetic: 35.6 us -> 19.2 us
    psum x1 -> x0, waiting for transfers between devices: 341 us -> none  [shards(): lax.psum(attn_partial.astype(jnp.bfloat16), 'head').astype(jnp.float32)]
    reduce_scatter x0 -> x1, waiting for transfers between devices: none -> 114 us  [shards(): lax.psum_scatter(attn_partial.astype(jnp.bfloat16), 'head', scatter_dimen...]
    all_gather x0 -> x1, waiting for transfers between devices: none -> 107 us  [shards(): normed = lax.all_gather(normed_rows, 'head', axis=1, tiled=True)]
    reduce_sum x2, other arithmetic: 9.9 us -> 3.45 us  [layer_norm(): center = values - jnp.mean(values, axis=-1, keepdims=True)]
    reduce_sum x2, other arithmetic: 10 us -> 3.72 us  [layer_norm(): spread = jnp.mean(center * center, axis=-1, keepdims=True)]
  transfers between devices with their start and end apart: 3 -> 4, of which waited for: 3 -> 4; matrix products, arithmetic and copies ran while one was open for 1% -> 1% of each run, Pallas kernels for 0% -> 0%
where the time goes in v2:
time: 485 us; the launch traced here: 484 us
  waiting for transfers between devices  365 us (75%)
  matrix products  65 us (13%)
  other arithmetic  19.2 us (4%)
  blocking collectives  14.5 us (3%)
  between operations  13.9 us (3%)
  local copies, waits for them, and re-layouts  6.2 us (1%)
    reduce_scatter x1, waiting for transfers between devices, shards(): lax.psum_scatter(attn_partial.astype(jnp.bfloat16), 'head', scatter_dimen...  114 us
    reduce_scatter x1, waiting for transfers between devices, shards(): lax.psum_scatter(mlp_partial.astype(jnp.bfloat16), 'head', scatter_dimens...  108 us
    all_gather x1, waiting for transfers between devices, shards(): normed = lax.all_gather(normed_rows, 'head', axis=1, tiled=True)  107 us
    all_gather x1, waiting for transfers between devices, regroup_weights(): whole = lax.all_gather(packed, 'seq', axis=0, tiled=True)  35.7 us
    dot_general x1, matrix products, shards(): jnp.einsum('plf,ef->ple', hidden, down_weight_t, preferred_element_type=j...  23.4 us
    all_to_all x1, blocking collectives, regroup_weights(): packed = lax.all_to_all(packed, 'head', 1, 0, tiled=True)  14.5 us
  transfers between devices with their start and end apart: 4, of which 4 were waited for; matrix products, arithmetic and copies ran while one was open for 1% of the time, Pallas kernels for 0%

profile of v2, /device:TPU:1, one launch (start us, length us, event | category | flops | bytes accessed | tf_op | source)
XLA Modules:
  0.0 484.0 jit_solution(16174309886386023024)
XLA Ops:
  7.2 0.0 all-gather.3.cloned.1.call-start
  7.2 0.8 convert_bitcast_fusion.2
  8.0 0.9 copy_bitcast_fusion
  8.9 0.9 convert_element_type.56
  9.8 0.9 convert_element_type.58
  10.7 14.5 %all_to_all.15 = bf16[8,8,1536]{2,0,1:T(8,128)(2,1)} all-to-all(bf16[8,8,1536]{2,0,1:T(8,128)(2,1)S(1)} %pad_maximum_fusion), channel_id=1, replica_groups=mesh['seq'=16,'head'=8] {'head'}, dimensions={1} | all-to-all | bytes 393216 | tf_op jit(solution)/shard_map/all_to_all | solution.py:32
  25.2 0.0 all-gather.3.cloned.1.call-update
  25.2 0.0 reduce-scatter.3.cloned.1.call-start
  25.3 0.7 iota_compare_fusion
  26.0 35.7 %all-gather.3.cloned.1.call-done = bf16[1024,1536]{1,0:T(8,128)(2,1)} async-done(((bf16[64,1536]{1,0:T(8,128)(2,1)}), bf16[1024,1536]{1,0:T(8,128)(2,1)}) %all-gather.3.cloned.1.call-update) | async-done | bytes 3145744 | tf_op jit(solution)/shard_map/all_gather | solution.py:34
  61.7 1.2 slice.44
  62.9 0.3 copy.12
  63.2 9.2 %convert_bitcast_fusion = bf16[8,512,3,128]{1,3,0,2:T(8,128)(2,1)S(1)} fusion(bf16[1024,3,128,1]{0,2,3,1:T(8,128)(2,1)S(1)} %bitcast.69, bf16[8,512,1024]{2,1,0:T(8,128)(2,1)} %param.8), kind=kOutput, calls=%fused_computation.66 | convolution fusion | flops 3222798336 | bytes 12320768 | tf_op jit(solution)/shard_map/pld,dte->plte/dot_general | solution.py:54
  72.4 0.0 copy-start.1
  72.4 1.7 copy-done.1
  74.0 0.3 fusion.96
  74.4 8.9 %fusion.99 = (f32[8,2,512]{2,1,0:T(2,128)S(1)}, f32[8,2,512,512]{2,3,1,0:T(8,128)}) fusion(pred[8,512]{1,0:T(8,128)(4,1)S(1)} %iota_compare_fusion, bf16[8,512,2,64]{1,3,2,0:T(8,128)(2,1)S(1)} %bitcast.68, bf16[8,512,2,64]{1,3,2,0:T(8,128)(2,1)S(1)} %bitcast.67), kind=kOutput, calls=%fused_computation.135 | convolution fusion | flops 553648640 | bytes 18911232 | tf_op jit(solution)/shard_map/sub | solution.py:69
  83.3 7.4 %fusion.59 = bf16[8,2,64,512]{3,2,1,0:T(8,128)(2,1)S(1)} fusion(bf16[8,512,2,64]{1,3,2,0:T(8,128)(2,1)S(1)} %bitcast.66, f32[8,2,512,512]{2,3,1,0:T(8,128)} %get-tuple-element.18, f32[8,2,512]{2,1,0:T(2,128)S(1)} %get-tuple-element.17), kind=kOutput, calls=%fused_computation.80 | convolution fusion | flops 545783808 | bytes 18907136 | tf_op jit(solution)/shard_map/phqk,pkhd->pqhd/dot_general | solution.py:71
  90.7 0.0 copy-start.3
  90.7 0.0 copy-start.4
  90.7 6.6 %convolution_convert_fusion = bf16[8,512,1024]{2,1,0:T(8,128)(2,1)} fusion(bf16[8,512,128]{1,2,0:T(8,128)(2,1)S(1)} %bitcast.65, bf16[1024,1536]{1,0:T(8,128)(2,1)} %all-gather.3.cloned.1.call-done), kind=kOutput, calls=%fused_computation.33 | convolution fusion | flops 1077936128 | bytes 9699328 | tf_op jit(solution)/shard_map/pld,ed->ple/dot_general | solution.py:79
  97.3 0.0 copy-start.2
  97.3 0.0 reduce-scatter.3.cloned.1.call-update
  97.3 0.0 all-gather.5.cloned.1.call-start
  97.3 0.0 copy-done.3
  97.4 0.0 copy-done.4
  97.4 114.0 %reduce-scatter.3.cloned.1.call-done = bf16[8,64,1024]{2,1,0:T(8,128)(2,1)} async-done(((bf16[8,512,1024]{2,1,0:T(8,128)(2,1)}), bf16[8,64,1024]{2,1,0:T(8,128)(2,1)}) %reduce-scatter.3.cloned.1.call-update) | async-done | bytes 1048592 | tf_op jit(solution)/shard_map/reduce_scatter | solution.py:82
  211.4 1.9 fusion.54
  213.3 2.0 multiply_reduce_fusion.1
  215.3 3.1 add_convert_fusion
  218.4 0.0 all-gather.5.cloned.1.call-update
  218.4 0.2 reduce-scatter.5.cloned.1.call-start
  218.6 106.7 %all-gather.5.cloned.1.call-done = bf16[8,512,1024]{2,1,0:T(8,128)(2,1)} async-done(((bf16[8,64,1024]{2,1,0:T(8,128)(2,1)}), bf16[8,512,1024]{2,1,0:T(8,128)(2,1)}) %all-gather.5.cloned.1.call-update) | async-done | bytes 8388624 | tf_op jit(solution)/shard_map/all_gather | solution.py:89
  325.4 0.0 copy-done.2
  325.4 9.6 %fusion.52 = (u8[512,512]{1,0:T(8,128)(4,1)S(1)}, u8[512,512]{1,0:T(8,128)(4,1)S(1)}, f32[8,512,512]{2,1,0:T(8,128)S(1)}) fusion(bf16[8,512,1024]{2,1,0:T(8,128)(2,1)} %all-gather.5.cloned.1.call-done, bf16[1024,1536]{1,0:T(8,128)(2,1)S(1)} %copy-done.2), kind=kOutput, calls=%fused_computation.74 | convolution fusion | flops 4321705984 | bytes 18350080 | tf_op jit(solution)/shard_map/pld,df->plf/dot_general | solution.py:91
  335.0 23.4 %convolution_convert_fusion.1 = bf16[8,512,1024]{2,1,0:T(8,128)(2,1)} fusion(f32[8,512,512]{2,1,0:T(8,128)S(1)} %get-tuple-element.19, u8[512,512]{1,0:T(8,128)(4,1)S(1)} %get-tuple-element.7, u8[512,512]{1,0:T(8,128)(4,1)S(1)} %get-tuple-element.6, bf16[1024,1536]{1,0:T(8,128)(2,1)S(1)} %copy-done.2), kind=kOutput, calls=%fused_computation.34 | convolution fusion | flops 4445962240 | bytes 18350080 | tf_op jit(solution)/shard_map/plf,ef->ple/dot_general | solution.py:94
  358.4 0.0 copy-start
  358.4 0.0 reduce-scatter.5.cloned.1.call-update
  358.4 0.1 constant_dynamic-slice_fusion
  358.5 1.8 bitcast_select_fusion
  360.2 1.3 copy.16
  361.5 1.3 copy.15
  362.8 108.4 %reduce-scatter.5.cloned.1.call-done = bf16[8,64,1024]{2,1,0:T(8,128)(2,1)} async-done(((bf16[8,512,1024]{2,1,0:T(8,128)(2,1)}), bf16[8,64,1024]{2,1,0:T(8,128)(2,1)}) %reduce-scatter.5.cloned.1.call-update) | async-done | bytes 1048592 | tf_op jit(solution)/shard_map/reduce_scatter | solution.py:95
  471.2 0.0 copy-done
  471.2 1.6 fusion.56
  472.8 1.7 multiply_reduce_fusion
  474.5 2.9 select_convert_fusion
  (7 shorter events, 0.1 us)
Async XLA Ops:
  7.2 54.5 %all-gather.3.cloned.1.call-start = ((), (), s32[]{:S(2)}) async-start(), calls=%async_computation.3 | async-start | bytes 3342336 | tf_op jit(solution)/shard_map/all_gather | solution.py:34
  25.2 186.2 %reduce-scatter.3.cloned.1.call-start = ((), (), s32[]{:S(2)}) async-start(), calls=%async_computation.4 | async-start | bytes 9437184 | tf_op jit(solution)/shard_map/reduce_scatter | solution.py:82
  72.4 1.7 copy-start.1
  90.7 6.7 %copy-start.3 = (f32[2,1024]{1,0:T(2,128)S(1)}, f32[2,1024]{1,0:T(2,128)}, u32[]{:S(2)}) copy-start(f32[2,1024]{1,0:T(2,128)} %param.14) | copy-start | bytes 24580
  90.7 6.7 %copy-start.4 = (f32[2,1024]{1,0:T(2,128)S(1)}, f32[2,1024]{1,0:T(2,128)}, u32[]{:S(2)}) copy-start(f32[2,1024]{1,0:T(2,128)} %param.15) | copy-start | bytes 24580
  97.3 228.1 %copy-start.2 = (bf16[1024,1536]{1,0:T(8,128)(2,1)S(1)}, bf16[1024,1536]{1,0:T(8,128)(2,1)}, u32[]{:S(2)}) copy-start(bf16[1024,1536]{1,0:T(8,128)(2,1)} %all-gather.3.cloned.1.call-done) | copy-start | bytes 9437188
  97.3 228.1 %all-gather.5.cloned.1.call-start = ((), (), s32[]{:S(2)}) async-start(), calls=%async_computation.5 | async-start | bytes 9437184 | tf_op jit(solution)/shard_map/all_gather | solution.py:89
  218.4 252.8 %reduce-scatter.5.cloned.1.call-start = ((), (), s32[]{:S(2)}) async-start(), calls=%async_computation.6 | async-start | bytes 9437184 | tf_op jit(solution)/shard_map/reduce_scatter | solution.py:95
  358.4 112.9 %copy-start = (bf16[8,64,1024]{2,1,0:T(8,128)(2,1)S(1)}, bf16[8,64,1024]{2,1,0:T(8,128)(2,1)}, u32[]{:S(2)}) copy-start(bf16[8,64,1024]{2,1,0:T(8,128)(2,1)} %add_convert_fusion) | copy-start | bytes 3145732
Sparse Core Ops, SparseCore 0:
  25.3 36.2 all-gather.2
  97.4 113.9 reduce-scatter.2
  218.5 106.7 all-gather.4
  358.5 112.6 reduce-scatter.4

commit v3 on v2

--- a/solution.py
+++ b/solution.py
@@ -17,28 +17,29 @@
     return center * lax.rsqrt(spread + EPSILON) * gain + shift
 
 
-def regroup_weights(attn_in, attn_out, mlp_in, mlp_out, heads_axis):
+def regroup_weights(attn_in, attn_out, heads_axis):
     rows = attn_in.shape[0]
     model_width = attn_in.shape[2]
-    hidden_width = mlp_in.shape[1]
     block_width = model_width // heads_axis
-    hidden_block = hidden_width // heads_axis
     in_piece = attn_in.astype(jnp.bfloat16).reshape(rows, 3, heads_axis, block_width)
     in_piece = jnp.transpose(in_piece, (0, 2, 1, 3)).reshape(rows, heads_axis, 3 * block_width)
-    up_piece = mlp_in.astype(jnp.bfloat16).reshape(rows, heads_axis, hidden_block)
     out_piece = attn_out.astype(jnp.bfloat16).T.reshape(rows, heads_axis, block_width)
-    down_piece = mlp_out.astype(jnp.bfloat16).T.reshape(rows, heads_axis, hidden_block)
-    packed = jnp.concatenate([in_piece, up_piece, out_piece, down_piece], axis=2)
+    packed = jnp.concatenate([in_piece, out_piece], axis=2)
     packed = lax.all_to_all(packed, "head", 1, 0, tiled=True)
     packed = packed.reshape(rows * heads_axis, packed.shape[2])
     whole = lax.all_gather(packed, "seq", axis=0, tiled=True)
-    edges = [0, 3 * block_width, 3 * block_width + hidden_block,
-             4 * block_width + hidden_block, 4 * block_width + 2 * hidden_block]
-    qkv_weight = whole[:, edges[0]:edges[1]].reshape(-1, 3, block_width)
-    up_weight = whole[:, edges[1]:edges[2]]
-    proj_weight_t = whole[:, edges[2]:edges[3]]
-    down_weight_t = whole[:, edges[3]:edges[4]]
-    return qkv_weight, up_weight, proj_weight_t, down_weight_t
+    qkv_weight = whole[:, :3 * block_width].reshape(-1, 3, block_width)
+    proj_weight_t = whole[:, 3 * block_width:]
+    return qkv_weight, proj_weight_t
+
+
+def gather_mlp(mlp_in, mlp_out):
+    hidden_width = mlp_in.shape[1]
+    packed = jnp.concatenate(
+        [mlp_in.astype(jnp.bfloat16), mlp_out.astype(jnp.bfloat16).T], axis=1)
+    packed = lax.all_gather(packed, "head", axis=0, tiled=True)
+    whole = lax.all_gather(packed, "seq", axis=0, tiled=True)
+    return whole[:, :hidden_width], whole[:, hidden_width:]
 
 
 def shards(tokens, lengths, attn_in, attn_out, mlp_in, mlp_out, norm_gain, norm_shift):
@@ -47,10 +48,12 @@
     prompts = tokens.shape[0]
     seq_len = tokens.shape[1]
     model_width = tokens.shape[2]
+    hidden_width = mlp_in.shape[1]
     block_width = model_width // heads_axis
+    hidden_block = hidden_width // heads_axis
     local_heads = block_width // DH
-    qkv_weight, up_weight, proj_weight_t, down_weight_t = regroup_weights(
-        attn_in, attn_out, mlp_in, mlp_out, heads_axis)
+    qkv_weight, proj_weight_t = regroup_weights(attn_in, attn_out, heads_axis)
+    up_weight, down_weight_t = gather_mlp(mlp_in, mlp_out)
     projected = jnp.einsum(
         "pld,dte->plte", tokens, qkv_weight, preferred_element_type=jnp.float32
     ).astype(jnp.bfloat16)
@@ -78,23 +81,24 @@
     row_start = head_index * row_count
     attn_partial = jnp.einsum(
         "pld,ed->ple", context, proj_weight_t, preferred_element_type=jnp.float32
-    )
-    attn_rows = lax.psum_scatter(
-        attn_partial.astype(jnp.bfloat16), "head", scatter_dimension=1, tiled=True
-    ).astype(jnp.float32)
+    ).astype(jnp.bfloat16)
+    attn_blocks = lax.all_to_all(
+        attn_partial.reshape(prompts, heads_axis, row_count, model_width), "head", 1, 1, tiled=True)
+    attn_rows = jnp.sum(attn_blocks.astype(jnp.float32), axis=1)
     token_rows = lax.dynamic_slice_in_dim(tokens, row_start, row_count, 1)
     normed_rows = layer_norm(
         token_rows.astype(jnp.float32) + attn_rows, norm_gain[0], norm_shift[0]
     ).astype(jnp.bfloat16)
-    normed = lax.all_gather(normed_rows, "head", axis=1, tiled=True)
     hidden = jax.nn.gelu(
-        jnp.einsum("pld,df->plf", normed, up_weight, preferred_element_type=jnp.float32),
+        jnp.einsum("pld,df->plf", normed_rows, up_weight, preferred_element_type=jnp.float32),
         approximate=False,
     ).astype(jnp.bfloat16)
-    mlp_partial = jnp.einsum("plf,ef->ple", hidden, down_weight_t, preferred_element_type=jnp.float32)
-    mlp_rows = lax.psum_scatter(
-        mlp_partial.astype(jnp.bfloat16), "head", scatter_dimension=1, tiled=True
-    ).astype(jnp.float32)
+    hidden = hidden.reshape(prompts, row_count, heads_axis, hidden_block)
+    down_blocks = down_weight_t.reshape(model_width, heads_axis, hidden_block)
+    mlp_blocks = jnp.einsum(
+        "plbf,ebf->plbe", hidden, down_blocks, preferred_element_type=jnp.float32
+    ).astype(jnp.bfloat16)
+    mlp_rows = jnp.sum(mlp_blocks.astype(jnp.float32), axis=2)
     finished = layer_norm(normed_rows.astype(jnp.float32) + mlp_rows, norm_gain[1], norm_shift[1])
     inside_rows = lax.dynamic_slice_in_dim(inside, row_start, row_count, 1)
     encoded = jnp.where(inside_rows[:, :, None], finished, 0.0).astype(jnp.bfloat16)

time: 485 us -> 333 us (0.69)
  waiting for transfers between devices: 365 us -> 183 us
  local copies, waits for them, and re-layouts: 6.2 us -> 27.7 us
  starting transfers between devices: 0.34 us -> 6.49 us
    reduce_scatter x2 -> x0, waiting for transfers between devices: 222 us -> none  [the longest x1 114 us: shards(): lax.psum_scatter(attn_partial.astype(jnp.bfloat16), 'head', scatter_dimen...]
    all_to_all x0 -> x1, waiting for transfers between devices: none -> 110 us  [shards(): lax.all_to_all(attn_partial.reshape(prompts, heads_axis, row_count, model...]
    all_gather x1 -> x2, waiting for transfers between devices: 107 us -> 39.2 us  [the longest x1 35 us: gather_mlp(): packed = lax.all_gather(packed, 'head', axis=0, tiled=True)]
    reshape x0 -> x2, local copies, waits for them, and re-layouts: none -> 11.1 us  [the longest x1 8.55 us: shards(): attn_partial.reshape(prompts, heads_axis, row_count, model_width)]
    unnamed x0 -> x1, matrix products: none -> 9.22 us
    dot_general x2 -> x1, matrix products: 33 us -> 23.8 us  [shards(): jnp.einsum('pld,df->plf', normed_rows, up_weight, preferred_element_type=...]
    slice x4 -> x5, local copies, waits for them, and re-layouts: 1.52 us -> 10.1 us  [the longest x1 7.71 us: gather_mlp(): return (whole[:, :hidden_width], whole[:, hidden_width:])]
    all_to_all x0 -> x1, starting transfers between devices: none -> 6.37 us  [shards(): lax.all_to_all(attn_partial.reshape(prompts, heads_axis, row_count, model...]
  transfers between devices with their start and end apart: 4 -> 4, of which waited for: 4 -> 4; matrix products, arithmetic and copies ran while one was open for 1% -> 19% of each run, Pallas kernels for 0% -> 0%
where the time goes in v3:
time: 333 us; the launch traced here: 332 us
  waiting for transfers between devices  183 us (55%)
  matrix products  65.5 us (20%)
  local copies, waits for them, and re-layouts  27.7 us (8%)
  other arithmetic  20.8 us (6%)
  blocking collectives  14 us (4%)
  between operations  13.9 us (4%)
  starting transfers between devices  6.49 us (2%)
    all_to_all x1, waiting for transfers between devices, shards(): lax.all_to_all(attn_partial.reshape(prompts, heads_axis, row_count, model...  110 us
    all_gather x1, waiting for transfers between devices, gather_mlp(): packed = lax.all_gather(packed, 'head', axis=0, tiled=True)  35 us
    all_gather x1, waiting for transfers between devices, regroup_weights(): whole = lax.all_gather(packed, 'seq', axis=0, tiled=True)  33.8 us
    dot_general x1, matrix products, shards(): jnp.einsum('pld,df->plf', normed_rows, up_weight, preferred_element_type=...  23.8 us
    all_to_all x1, blocking collectives, regroup_weights(): packed = lax.all_to_all(packed, 'head', 1, 0, tiled=True)  14 us
    sub x1, matrix products, shards(): raised = jnp.exp(scores - row_peak)  10.7 us
    unnamed x1, matrix products  9.22 us
    reshape x1, local copies, waits for them, and re-layouts, shards(): attn_partial.reshape(prompts, heads_axis, row_count, model_width)  8.55 us
  transfers between devices with their start and end apart: 4, of which 4 were waited for; matrix products, arithmetic and copies ran while one was open for 19% of the time, Pallas kernels for 0%

profile of v3, /device:TPU:1, one launch (start us, length us, event | category | flops | bytes accessed | tf_op | source)
XLA Modules:
  0.0 331.7 jit_solution(15236345032497120351)
XLA Ops:
  7.2 0.0 all-gather.6.cloned.1.call-start
  7.2 0.9 convert_bitcast_fusion.1
  8.1 0.9 convert_element_type.68
  9.0 0.7 pad_maximum_fusion
  9.7 0.0 all-gather.6.cloned.1.call-update
  9.7 0.0 all-gather.4.cloned.1.call-start
  9.8 0.8 convert_bitcast_fusion.3
  10.5 0.9 copy_bitcast_fusion.1
  11.4 14.0 %all_to_all.20 = bf16[8,8,512]{2,0,1:T(8,128)(2,1)} all-to-all(bf16[8,8,512]{2,0,1:T(8,128)(2,1)S(1)} %pad_maximum_fusion.1), channel_id=1, replica_groups=mesh['seq'=16,'head'=8] {'head'}, dimensions={1} | all-to-all | bytes 131072 | tf_op jit(solution)/shard_map/all_to_all | solution.py:28
  25.4 0.0 all-gather.4.cloned.1.call-update
  25.5 0.0 all-gather.8.cloned.1.call-start
  25.5 35.0 %all-gather.6.cloned.1.call-done = bf16[64,8192]{1,0:T(8,128)(2,1)} async-done(((bf16[8,8192]{1,0:T(8,128)(2,1)}), bf16[64,8192]{1,0:T(8,128)(2,1)}) %all-gather.6.cloned.1.call-update) | async-done | bytes 1048592 | tf_op jit(solution)/shard_map/all_gather | solution.py:40
  60.5 0.0 all-gather.8.cloned.1.call-update
  60.6 0.7 iota_compare_fusion
  61.3 33.8 %all-gather.4.cloned.1.call-done = bf16[1024,512]{1,0:T(8,128)(2,1)} async-done(((bf16[64,512]{1,0:T(8,128)(2,1)}), bf16[1024,512]{1,0:T(8,128)(2,1)}) %all-gather.4.cloned.1.call-update) | async-done | bytes 1048592 | tf_op jit(solution)/shard_map/all_gather | solution.py:30
  95.0 1.2 slice.44
  96.3 1.2 copy.20
  97.4 7.1 %convert_bitcast_fusion = bf16[8,512,3,128]{1,3,0,2:T(8,128)(2,1)S(1)} fusion(bf16[1024,3,128,1]{0,2,3,1:T(8,128)(2,1)} %bitcast.97, bf16[8,512,1024]{2,1,0:T(8,128)(2,1)} %param.8), kind=kOutput, calls=%fused_computation.40 | convolution fusion | flops 3222798336 | bytes 12320768 | tf_op jit(solution)/shard_map/pld,dte->plte/dot_general | solution.py:57
  104.5 1.8 fusion.35
  106.3 10.7 %fusion.38 = (f32[8,2,512]{2,1,0:T(2,128)S(1)}, f32[8,2,512,512]{2,3,1,0:T(8,128)}) fusion(pred[8,512]{1,0:T(8,128)(4,1)S(1)} %iota_compare_fusion, bf16[8,512,2,64]{1,3,2,0:T(8,128)(2,1)} %bitcast.96, bf16[8,512,2,64]{1,3,2,0:T(8,128)(2,1)} %bitcast.95), kind=kOutput, calls=%fused_computation.71 | convolution fusion | flops 553648640 | bytes 18911232 | tf_op jit(solution)/shard_map/sub | solution.py:72
  117.1 8.0 %fusion.30 = bf16[8,2,64,512]{3,2,1,0:T(8,128)(2,1)S(1)} fusion(bf16[8,512,2,64]{1,3,2,0:T(8,128)(2,1)} %bitcast.94, f32[8,2,512,512]{2,3,1,0:T(8,128)} %get-tuple-element.19, f32[8,2,512]{2,1,0:T(2,128)S(1)} %get-tuple-element.18), kind=kOutput, calls=%fused_computation.48 | convolution fusion | flops 545783808 | bytes 18907136 | tf_op jit(solution)/shard_map/phqk,pkhd->pqhd/dot_general | solution.py:74
  125.1 6.6 %convolution_convert_fusion = bf16[8,512,1024]{2,1,0:T(8,128)(2,1)} fusion(bf16[8,512,128]{1,2,0:T(8,128)(2,1)S(1)} %bitcast.93, bf16[1024,512]{1,0:T(8,128)(2,1)} %all-gather.4.cloned.1.call-done), kind=kOutput, calls=%fused_computation.38 | convolution fusion | flops 1077936128 | bytes 9699328 | tf_op jit(solution)/shard_map/pld,ed->ple/dot_general | solution.py:82
  131.7 8.6 %copy.23 = bf16[8,8,64,1024]{3,2,0,1:T(8,128)(2,1)} copy(bf16[8,8,64,1024]{3,2,1,0:T(8,128)(2,1)} %bitcast.89) | data formatting | bytes 16777216 | tf_op jit(solution)/shard_map/reshape | solution.py:86
  140.2 0.0 copy-start
  140.2 0.0 copy-start.1
  140.2 6.4 %all-to-all-start.1 = ((bf16[8,8,64,1024]{3,2,0,1:T(8,128)(2,1)}), bf16[8,8,64,1024]{3,2,0,1:T(8,128)(2,1)}, u32[]{:S(2)}, u32[]{:S(2)}) async-start(bf16[8,8,64,1024]{3,2,0,1:T(8,128)(2,1)} %copy.23), calls=%async_computation.1 | async-start | bytes 16777216 | tf_op jit(solution)/shard_map/all_to_all | solution.py:85
  146.6 0.1 constant_dynamic-slice_fusion
  146.7 0.0 copy-done
  146.7 0.0 copy-done.1
  146.7 1.5 bitcast_select_fusion
  148.2 2.3 copy.26
  150.4 2.3 copy.27
  152.7 110.4 %all-to-all-done.1 = bf16[8,8,64,1024]{3,2,0,1:T(8,128)(2,1)} async-done(((bf16[8,8,64,1024]{3,2,0,1:T(8,128)(2,1)}), bf16[8,8,64,1024]{3,2,0,1:T(8,128)(2,1)}, u32[]{:S(2)}, u32[]{:S(2)}) %all-to-all-start.1) | async-done | bytes 8388640 | tf_op jit(solution)/shard_map/all_to_all | solution.py:85
  263.1 5.7 %convert_reduce_fusion.1 = f32[8,64,1024]{2,1,0:T(8,128)S(1)} fusion(bf16[8,8,64,1024]{3,2,0,1:T(8,128)(2,1)} %all-to-all-done.1), kind=kLoop, calls=%fused_computation.3 | loop fusion | flops 7864320 | bytes 10485760 | tf_op jit(solution)/shard_map/reduce_sum | solution.py:87
  268.9 1.5 fusion.32
  270.4 1.7 multiply_reduce_fusion.1
  272.1 1.7 add_convert_fusion
  273.8 4.2 %all-gather.8.cloned.1.call-done = bf16[1024,8192]{1,0:T(8,128)(2,1)} async-done(((bf16[64,8192]{1,0:T(8,128)(2,1)}), bf16[1024,8192]{1,0:T(8,128)(2,1)}) %all-gather.8.cloned.1.call-update) | async-done | bytes 16777232 | tf_op jit(solution)/shard_map/all_gather | solution.py:41
  278.0 23.8 %fusion.4 = bf16[8,64,4096]{2,1,0:T(8,128)(2,1)S(1)} fusion(bf16[8,64,1024]{2,1,0:T(8,128)(2,1)S(1)} %add_convert_fusion, bf16[1024,8192]{1,0:T(8,128)(2,1)} %all-gather.8.cloned.1.call-done), kind=kOutput, calls=%fused_computation.11 | convolution fusion | flops 4431282176 | bytes 13631488 | tf_op jit(solution)/shard_map/pld,df->plf/dot_general | solution.py:93
  301.9 2.6 copy.43
  304.5 7.7 %slice.49 = bf16[1024,4096]{1,0:T(8,128)(2,1)} slice(bf16[1024,8192]{1,0:T(8,128)(2,1)} %all-gather.8.cloned.1.call-done), slice={[0:1024], [4096:8192]} | slice | bytes 16777216 | tf_op jit(solution)/shard_map/slice | solution.py:42
  312.2 9.2 %convert_reduce_fusion = f32[1024,8,64]{0,2,1:T(8,128)S(1)} fusion(bf16[8,512,512]{1,2,0:T(8,128)(2,1)} %bitcast.91, bf16[128,8,8,512]{3,2,1,0:T(8,128)(2,1)} %bitcast.90), kind=kOutput, calls=%fused_computation.2 | convolution fusion | flops 4307025920 | bytes 14680064
  321.4 0.3 fusion.31
  321.7 0.4 multiply_reduce_fusion
  322.1 3.1 select_convert_fusion
  (7 shorter events, 0.0 us)
Async XLA Ops:
  7.2 53.4 %all-gather.6.cloned.1.call-start = ((), (), s32[]{:S(2)}) async-start(), calls=%async_computation.3 | async-start | bytes 1179648 | tf_op jit(solution)/shard_map/all_gather | solution.py:40
  9.7 85.3 %all-gather.4.cloned.1.call-start = ((), (), s32[]{:S(2)}) async-start(), calls=%async_computation.2 | async-start | bytes 1114112 | tf_op jit(solution)/shard_map/all_gather | solution.py:30
  25.5 252.6 %all-gather.8.cloned.1.call-start = ((), (), s32[]{:S(2)}) async-start(), calls=%async_computation.4 | async-start | bytes 17825792 | tf_op jit(solution)/shard_map/all_gather | solution.py:41
  140.2 6.5 %copy-start = (f32[2,1024]{1,0:T(2,128)S(1)}, f32[2,1024]{1,0:T(2,128)}, u32[]{:S(2)}) copy-start(f32[2,1024]{1,0:T(2,128)} %param.15) | copy-start | bytes 24580
  140.2 6.5 %copy-start.1 = (f32[2,1024]{1,0:T(2,128)S(1)}, f32[2,1024]{1,0:T(2,128)}, u32[]{:S(2)}) copy-start(f32[2,1024]{1,0:T(2,128)} %param.14) | copy-start | bytes 24580
  140.2 122.9 %all-to-all-start.1 = ((bf16[8,8,64,1024]{3,2,0,1:T(8,128)(2,1)}), bf16[8,8,64,1024]{3,2,0,1:T(8,128)(2,1)}, u32[]{:S(2)}, u32[]{:S(2)}) async-start(bf16[8,8,64,1024]{3,2,0,1:T(8,128)(2,1)} %copy.23), calls=%async_computation.1 | async-start | bytes 16777216 | tf_op jit(solution)/shard_map/all_to_all | solution.py:85
Sparse Core Ops, SparseCore 0:
  10.9 49.5 all-gather.5
  62.2 32.7 all-gather.3
  96.8 181.2 all-gather.7

commit v4 on v3

--- a/solution.py
+++ b/solution.py
@@ -17,29 +17,28 @@
     return center * lax.rsqrt(spread + EPSILON) * gain + shift
 
 
-def regroup_weights(attn_in, attn_out, heads_axis):
+def regroup_weights(attn_in, attn_out, mlp_in, mlp_out, heads_axis, seq_axis):
     rows = attn_in.shape[0]
     model_width = attn_in.shape[2]
+    hidden_width = mlp_in.shape[1]
     block_width = model_width // heads_axis
     in_piece = attn_in.astype(jnp.bfloat16).reshape(rows, 3, heads_axis, block_width)
     in_piece = jnp.transpose(in_piece, (0, 2, 1, 3)).reshape(rows, heads_axis, 3 * block_width)
     out_piece = attn_out.astype(jnp.bfloat16).T.reshape(rows, heads_axis, block_width)
-    packed = jnp.concatenate([in_piece, out_piece], axis=2)
+    mlp_rows = jnp.concatenate(
+        [mlp_in.astype(jnp.bfloat16), mlp_out.astype(jnp.bfloat16).T], axis=1)
+    mlp_piece = jnp.broadcast_to(mlp_rows[:, None], (rows, heads_axis, 2 * hidden_width))
+    packed = jnp.concatenate([in_piece, out_piece, mlp_piece], axis=2)
     packed = lax.all_to_all(packed, "head", 1, 0, tiled=True)
     packed = packed.reshape(rows * heads_axis, packed.shape[2])
-    whole = lax.all_gather(packed, "seq", axis=0, tiled=True)
-    qkv_weight = whole[:, :3 * block_width].reshape(-1, 3, block_width)
-    proj_weight_t = whole[:, 3 * block_width:]
-    return qkv_weight, proj_weight_t
-
-
-def gather_mlp(mlp_in, mlp_out):
-    hidden_width = mlp_in.shape[1]
-    packed = jnp.concatenate(
-        [mlp_in.astype(jnp.bfloat16), mlp_out.astype(jnp.bfloat16).T], axis=1)
-    packed = lax.all_gather(packed, "head", axis=0, tiled=True)
-    whole = lax.all_gather(packed, "seq", axis=0, tiled=True)
-    return whole[:, :hidden_width], whole[:, hidden_width:]
+    attn_part = packed[:, :4 * block_width]
+    attn_part = jnp.broadcast_to(attn_part[None], (seq_axis,) + attn_part.shape)
+    attn_whole = lax.all_to_all(attn_part, "seq", 0, 0, tiled=True)
+    attn_whole = attn_whole.reshape(-1, 4 * block_width)
+    qkv_weight = attn_whole[:, :3 * block_width].reshape(-1, 3, block_width)
+    proj_weight_t = attn_whole[:, 3 * block_width:]
+    mlp_whole = lax.all_gather(packed[:, 4 * block_width:], "seq", axis=0, tiled=True)
+    return qkv_weight, proj_weight_t, mlp_whole[:, :hidden_width], mlp_whole[:, hidden_width:]
 
 
 def shards(tokens, lengths, attn_in, attn_out, mlp_in, mlp_out, norm_gain, norm_shift):
@@ -52,8 +51,8 @@
     block_width = model_width // heads_axis
     hidden_block = hidden_width // heads_axis
     local_heads = block_width // DH
-    qkv_weight, proj_weight_t = regroup_weights(attn_in, attn_out, heads_axis)
-    up_weight, down_weight_t = gather_mlp(mlp_in, mlp_out)
+    qkv_weight, proj_weight_t, up_weight, down_weight_t = regroup_weights(
+        attn_in, attn_out, mlp_in, mlp_out, heads_axis, lax.axis_size("seq"))
     projected = jnp.einsum(
         "pld,dte->plte", tokens, qkv_weight, preferred_element_type=jnp.float32
     ).astype(jnp.bfloat16)

time: 333 us -> 303 us (0.910)
  waiting for transfers between devices: 183 us -> 137 us
  blocking collectives: 14 us -> 24.1 us
  starting transfers between devices: 6.49 us -> 12.9 us
    all_gather x3 -> x1, waiting for transfers between devices: 73 us -> 0.02 us  [regroup_weights(): lax.all_gather(packed[:, 4 * block_width:], 'seq', axis=0, tiled=True)]
    all_to_all x0 -> x1, waiting for transfers between devices: none -> 27.2 us  [regroup_weights(): attn_whole = lax.all_to_all(attn_part, 'seq', 0, 0, tiled=True)]
    all_to_all x1, blocking collectives: 14 us -> 24.1 us  [regroup_weights(): packed = lax.all_to_all(packed, 'head', 1, 0, tiled=True)]
    all_to_all x0 -> x1, starting transfers between devices: none -> 7.57 us  [regroup_weights(): attn_whole = lax.all_to_all(attn_part, 'seq', 0, 0, tiled=True)]
    slice x3 -> x5, local copies, waits for them, and re-layouts: 10.1 us -> 10 us  [the longest x1 7.71 us: regroup_weights(): mlp_whole[:, hidden_width:]]
  transfers between devices with their start and end apart: 4 -> 3, of which waited for: 4 -> 2; matrix products, arithmetic and copies ran while one was open for 19% -> 21% of each run, Pallas kernels for 0% -> 0%
where the time goes in v4:
time: 303 us; the launch traced here: 302 us
  waiting for transfers between devices  137 us (45%)
  matrix products  65.7 us (22%)
  local copies, waits for them, and re-layouts  28.7 us (9%)
  blocking collectives  24.1 us (8%)
  other arithmetic  19.6 us (6%)
  between operations  14.2 us (5%)
  starting transfers between devices  12.9 us (4%)
    all_to_all x1, waiting for transfers between devices, shards(): lax.all_to_all(attn_partial.reshape(prompts, heads_axis, row_count, model...  109 us
    all_to_all x1, waiting for transfers between devices, regroup_weights(): attn_whole = lax.all_to_all(attn_part, 'seq', 0, 0, tiled=True)  27.2 us
    all_to_all x1, blocking collectives, regroup_weights(): packed = lax.all_to_all(packed, 'head', 1, 0, tiled=True)  24.1 us
    dot_general x1, matrix products, shards(): jnp.einsum('pld,df->plf', normed_rows, up_weight, preferred_element_type=...  23.8 us
    sub x1, matrix products, shards(): raised = jnp.exp(scores - row_peak)  10.8 us
    unnamed x1, matrix products  9.23 us
    reshape x1, local copies, waits for them, and re-layouts, shards(): attn_partial.reshape(prompts, heads_axis, row_count, model_width)  8.55 us
    dot_general x1, matrix products, shards(): jnp.einsum('phqk,pkhd->pqhd', weights, value_heads, preferred_element_typ...  8.03 us
  transfers between devices with their start and end apart: 3, of which 2 were waited for; matrix products, arithmetic and copies ran while one was open for 21% of the time, Pallas kernels for 0%

profile of v4, /device:TPU:1, one launch (start us, length us, event | category | flops | bytes accessed | tf_op | source)
XLA Modules:
  0.0 301.7 jit_solution(6259269138191719484)
XLA Ops:
  7.2 0.0 copy-start.3
  7.2 0.0 all-gather.2.cloned.1.call-start
  7.2 0.9 convert_bitcast_fusion.1
  8.1 0.9 convert_element_type.59
  9.0 0.8 convert_bitcast_fusion.3
  9.8 0.9 copy_bitcast_fusion.1
  10.7 0.1 broadcast_in_dim.36
  10.8 0.1 pad_maximum_fusion
  10.9 24.1 %all_to_all.25 = bf16[8,8,8704]{2,0,1:T(8,128)(2,1)S(1)} all-to-all(bf16[8,8,8704]{2,0,1:T(8,128)(2,1)S(1)} %pad_maximum_fusion), channel_id=1, replica_groups=mesh['seq'=16,'head'=8] {'head'}, dimensions={1} | all-to-all | bytes 2228224 | tf_op jit(solution)/shard_map/all_to_all | solution.py:32
  35.0 1.1 slice.58
  36.1 0.0 all-gather.2.cloned.1.call-update
  36.1 1.1 broadcast_in_dim.37
  37.2 7.6 %all-to-all-start.1 = ((bf16[16,64,512]{2,1,0:T(8,128)(2,1)}), bf16[16,64,512]{2,1,0:T(8,128)(2,1)S(1)}, u32[]{:S(2)}, u32[]{:S(2)}) async-start(bf16[16,64,512]{2,1,0:T(8,128)(2,1)} %broadcast_in_dim.37), calls=%async_computation.1 | async-start | bytes 2097152 | tf_op jit(solution)/shard_map/all_to_all | solution.py:36
  44.7 0.0 copy-done.3
  44.7 0.1 iota_compare_fusion
  44.8 27.2 %all-to-all-done.1 = bf16[16,64,512]{2,1,0:T(8,128)(2,1)S(1)} async-done(((bf16[16,64,512]{2,1,0:T(8,128)(2,1)}), bf16[16,64,512]{2,1,0:T(8,128)(2,1)S(1)}, u32[]{:S(2)}, u32[]{:S(2)}) %all-to-all-start.1) | async-done | bytes 1048608 | tf_op jit(solution)/shard_map/all_to_all | solution.py:36
  72.1 0.0 copy-start
  72.1 0.1 slice.53
  72.2 1.2 copy.20
  73.3 0.0 copy-done
  73.3 7.3 %convert_bitcast_fusion = bf16[8,512,3,128]{1,3,0,2:T(8,128)(2,1)S(1)} fusion(bf16[1024,3,128,1]{0,2,3,1:T(8,128)(2,1)} %bitcast.102, bf16[8,512,1024]{2,1,0:T(8,128)(2,1)} %param.8), kind=kOutput, calls=%fused_computation.40 | convolution fusion | flops 3222798336 | bytes 12320768 | tf_op jit(solution)/shard_map/pld,dte->plte/dot_general | solution.py:56
  80.6 1.8 fusion.35
  82.4 10.8 %fusion.38 = (f32[8,2,512]{2,1,0:T(2,128)S(1)}, f32[8,2,512,512]{2,3,1,0:T(8,128)}) fusion(pred[8,512]{1,0:T(8,128)(4,1)S(1)} %iota_compare_fusion, bf16[8,512,2,64]{1,3,2,0:T(8,128)(2,1)} %bitcast.101, bf16[8,512,2,64]{1,3,2,0:T(8,128)(2,1)} %bitcast.100), kind=kOutput, calls=%fused_computation.71 | convolution fusion | flops 553648640 | bytes 18911232 | tf_op jit(solution)/shard_map/sub | solution.py:71
  93.1 8.0 %fusion.30 = bf16[8,2,64,512]{3,2,1,0:T(8,128)(2,1)S(1)} fusion(bf16[8,512,2,64]{1,3,2,0:T(8,128)(2,1)} %bitcast.99, f32[8,2,512,512]{2,3,1,0:T(8,128)} %get-tuple-element.19, f32[8,2,512]{2,1,0:T(2,128)S(1)} %get-tuple-element.18), kind=kOutput, calls=%fused_computation.48 | convolution fusion | flops 545783808 | bytes 18907136 | tf_op jit(solution)/shard_map/phqk,pkhd->pqhd/dot_general | solution.py:73
  101.2 6.6 %convolution_convert_fusion = bf16[8,512,1024]{2,1,0:T(8,128)(2,1)} fusion(bf16[8,512,128]{1,2,0:T(8,128)(2,1)S(1)} %bitcast.98, bf16[1024,512]{1,0:T(8,128)(2,1)} %bitcast.95), kind=kOutput, calls=%fused_computation.38 | convolution fusion | flops 1077936128 | bytes 9699328 | tf_op jit(solution)/shard_map/pld,ed->ple/dot_general | solution.py:81
  107.7 8.6 %copy.23 = bf16[8,8,64,1024]{3,2,0,1:T(8,128)(2,1)} copy(bf16[8,8,64,1024]{3,2,1,0:T(8,128)(2,1)} %bitcast.90) | data formatting | bytes 16777216 | tf_op jit(solution)/shard_map/reshape | solution.py:85
  116.3 0.0 copy-start.1
  116.3 0.0 copy-start.2
  116.3 5.3 %all-to-all-start.2 = ((bf16[8,8,64,1024]{3,2,0,1:T(8,128)(2,1)}), bf16[8,8,64,1024]{3,2,0,1:T(8,128)(2,1)}, u32[]{:S(2)}, u32[]{:S(2)}) async-start(bf16[8,8,64,1024]{3,2,0,1:T(8,128)(2,1)} %copy.23), calls=%async_computation.2 | async-start | bytes 16777216 | tf_op jit(solution)/shard_map/all_to_all | solution.py:84
  121.6 0.1 constant_dynamic-slice_fusion
  121.7 0.0 copy-done.1
  121.7 0.0 copy-done.2
  121.7 1.5 bitcast_select_fusion
  123.2 2.3 copy.26
  125.5 2.3 copy.27
  127.7 109.2 %all-to-all-done.2 = bf16[8,8,64,1024]{3,2,0,1:T(8,128)(2,1)} async-done(((bf16[8,8,64,1024]{3,2,0,1:T(8,128)(2,1)}), bf16[8,8,64,1024]{3,2,0,1:T(8,128)(2,1)}, u32[]{:S(2)}, u32[]{:S(2)}) %all-to-all-start.2) | async-done | bytes 8388640 | tf_op jit(solution)/shard_map/all_to_all | solution.py:84
  236.9 5.7 %convert_reduce_fusion.1 = f32[8,64,1024]{2,1,0:T(8,128)S(1)} fusion(bf16[8,8,64,1024]{3,2,0,1:T(8,128)(2,1)} %all-to-all-done.2), kind=kLoop, calls=%fused_computation.3 | loop fusion | flops 7864320 | bytes 10485760 | tf_op jit(solution)/shard_map/reduce_sum | solution.py:86
  242.6 1.5 fusion.32
  244.2 1.7 multiply_reduce_fusion.1
  245.9 1.8 add_convert_fusion
  247.7 0.0 all-gather.2.cloned.1.call-done
  247.7 23.8 %fusion.4 = bf16[8,64,4096]{2,1,0:T(8,128)(2,1)S(1)} fusion(bf16[8,64,1024]{2,1,0:T(8,128)(2,1)S(1)} %add_convert_fusion, bf16[1024,8192]{1,0:T(8,128)(2,1)} %all-gather.2.cloned.1.call-done), kind=kOutput, calls=%fused_computation.11 | convolution fusion | flops 4431282176 | bytes 13631488 | tf_op jit(solution)/shard_map/pld,df->plf/dot_general | solution.py:92
  271.5 2.6 copy.43
  274.1 7.7 %slice.59 = bf16[1024,4096]{1,0:T(8,128)(2,1)} slice(bf16[1024,8192]{1,0:T(8,128)(2,1)} %all-gather.2.cloned.1.call-done), slice={[0:1024], [4096:8192]} | slice | bytes 16777216 | tf_op jit(solution)/shard_map/slice | solution.py:41
  281.8 9.2 %convert_reduce_fusion = f32[1024,8,64]{0,2,1:T(8,128)S(1)} fusion(bf16[8,512,512]{1,2,0:T(8,128)(2,1)} %bitcast.96, bf16[128,8,8,512]{3,2,1,0:T(8,128)(2,1)} %bitcast.91), kind=kOutput, calls=%fused_computation.2 | convolution fusion | flops 4307025920 | bytes 14680064
  291.1 0.3 fusion.31
  291.4 0.4 multiply_reduce_fusion
  291.8 3.1 %select_convert_fusion = bf16[8,64,1024]{2,1,0:T(8,128)(2,1)} fusion(f32[1024]{0:T(1024)S(1)} %bitcast.103, f32[1024]{0:T(1024)S(1)} %bitcast.104, f32[8,64]{1,0:T(8,128)S(1)} %add_rsqrt_fusion, f32[8,64]{1,0:T(8,128)S(1)} %broadcast_multiply_fusion, pred[8,64]{1,0:T(8,128)(4,1)S(1)} %constant_dynamic-slice_fusion, ...), kind=kLoop, calls=%fused_computation.42 | loop fusion | flops 4194304 | bytes 4207104 | tf_op jit(solution)/shard_map/convert_element_type | solution.py:103
  (8 shorter events, 0.1 us)
Async XLA Ops:
  7.2 37.6 %copy-start.3 = (s32[8]{0:T(128)S(1)}, s32[8]{0:T(128)}, u32[]{:S(2)}) copy-start(s32[8]{0:T(128)} %param.9) | copy-start | bytes 100
  7.2 240.5 %all-gather.2.cloned.1.call-start = ((), (), s32[]{:S(2)}) async-start(), calls=%async_computation.3 | async-start | bytes 17825792 | tf_op jit(solution)/shard_map/all_gather | solution.py:40
  37.2 34.9 %all-to-all-start.1 = ((bf16[16,64,512]{2,1,0:T(8,128)(2,1)}), bf16[16,64,512]{2,1,0:T(8,128)(2,1)S(1)}, u32[]{:S(2)}, u32[]{:S(2)}) async-start(bf16[16,64,512]{2,1,0:T(8,128)(2,1)} %broadcast_in_dim.37), calls=%async_computation.1 | async-start | bytes 2097152 | tf_op jit(solution)/shard_map/all_to_all | solution.py:36
  72.1 1.3 copy-start
  116.3 5.4 %copy-start.1 = (f32[2,1024]{1,0:T(2,128)S(1)}, f32[2,1024]{1,0:T(2,128)}, u32[]{:S(2)}) copy-start(f32[2,1024]{1,0:T(2,128)} %param.15) | copy-start | bytes 24580
  116.3 5.4 %copy-start.2 = (f32[2,1024]{1,0:T(2,128)S(1)}, f32[2,1024]{1,0:T(2,128)}, u32[]{:S(2)}) copy-start(f32[2,1024]{1,0:T(2,128)} %param.14) | copy-start | bytes 24580
  116.3 120.6 %all-to-all-start.2 = ((bf16[8,8,64,1024]{3,2,0,1:T(8,128)(2,1)}), bf16[8,8,64,1024]{3,2,0,1:T(8,128)(2,1)}, u32[]{:S(2)}, u32[]{:S(2)}) async-start(bf16[8,8,64,1024]{3,2,0,1:T(8,128)(2,1)} %copy.23), calls=%async_computation.2 | async-start | bytes 16777216 | tf_op jit(solution)/shard_map/all_to_all | solution.py:84
Sparse Core Ops, SparseCore 0:
  36.2 186.3 all-gather.1
